TPU v7x, 32 devices: a whole 2x2x4 slice. The times are simulated.
32 devices in a mesh: dp: 8 (over y, x, core), fsdp: 4 (over z).
Axes of the slice: x: 2, y: 2, z: 4, core: 2. Of those that a mesh axis runs over, the one named last changes fastest.
Arguments:
- inputs: bfloat16 [32, 8, 12, 6, 6, 256], P(('dp', 'fsdp')), may hold values from -6 to 6
- cotangent: bfloat16 [32, 8, 12, 6, 6, 256], P(('dp', 'fsdp')), may hold values from -6 to 6
- lengths: int32 [32], P(('dp', 'fsdp')), may hold values from 2 to 8
- face_table: int32 [12, 4], replicated, may hold values from 0 to 11
- w_first: float32 [2304, 256], P('fsdp'), may hold values from -0.125 to 0.125
- w_second: float32 [2304, 256], P('fsdp'), may hold values from -0.125 to 0.125
- w_skip: float32 [256, 256], P('fsdp'), may hold values from -0.375 to 0.375
- mom_first: float32 [2304, 256], P('fsdp'), may hold values from -64 to 64
- sq_first: float32 [2304, 256], P('fsdp'), may hold values from 12.16512 to 48.66048
- mom_second: float32 [2304, 256], P('fsdp'), may hold values from -64 to 64
- sq_second: float32 [2304, 256], P('fsdp'), may hold values from 12.16512 to 48.66048
- mom_skip: float32 [256, 256], P('fsdp'), may hold values from -160 to 160
- sq_skip: float32 [256, 256], P('fsdp'), may hold values from 68.56704 to 276.48
Outputs:
- output: bfloat16 [32, 8, 12, 6, 6, 256], P(('dp', 'fsdp'))
- grad_inputs: float32 [32, 8, 12, 6, 6, 256], P(('dp', 'fsdp'))
- new_first: float32 [2304, 256], P('fsdp')
- new_mom_first: float32 [2304, 256], P('fsdp')
- new_sq_first: float32 [2304, 256], P('fsdp')
- new_second: float32 [2304, 256], P('fsdp')
- new_mom_second: float32 [2304, 256], P('fsdp')
- new_sq_second: float32 [2304, 256], P('fsdp')
- new_skip: float32 [256, 256], P('fsdp')
- new_mom_skip: float32 [256, 256], P('fsdp')
- new_sq_skip: float32 [256, 256], P('fsdp')
All inputs are finite; a program needn't handle non-finite values.
Results may differ from a plain program's by a relative error of at most 0.019.
Values may be sent and summed in bfloat16 or wider, within the bound.
No kernel may reach another device: no remote copies, remote signals or barrier semaphores. Data moves between devices by JAX's collectives and lax.ppermute only.
A program may use at most 256 MiB of HBM per device.

v0:
```python
import jax
import jax.numpy as jnp
from jax import lax
from jax.sharding import PartitionSpec as P

C = 256
STEP_COUNT = 10
tap_offsets = [(row_off, col_off) for row_off in range(3) for col_off in range(3)]


def face_hots(face_table, dtype):
    faces = face_table.shape[0]
    labels = jnp.arange(faces, dtype=jnp.int32)
    return [
        (face_table[:, corner_side][:, None] == labels[None, :]).astype(dtype)
        for corner_side in range(4)
    ]


def pad_faces(field, hots):

    def route(matrix, edge, form):
        return jnp.einsum(form, matrix, edge, preferred_element_type=jnp.float32).astype(
            jnp.bfloat16
        )

    north = route(hots[0], field[:, :, -1], "fh,rhwc->rfwc")
    east = route(hots[1], field[:, :, :, 0], "fh,rhwc->rfwc")
    south = route(hots[2], field[:, :, 0], "fh,rhwc->rfwc")
    west = route(hots[3], field[:, :, :, -1], "fh,rhwc->rfwc")
    middle = jnp.concatenate([west[:, :, :, None], field, east[:, :, :, None]], axis=3)
    top_row = jnp.pad(north, ((0, 0), (0, 0), (1, 1), (0, 0)))
    bottom_row = jnp.pad(south, ((0, 0), (0, 0), (1, 1), (0, 0)))
    return jnp.concatenate([top_row[:, :, None], middle, bottom_row[:, :, None]], axis=2)


def unpad_back(spread, hots):
    highest = lax.Precision.HIGHEST
    inner = spread[:, :, 1:-1, 1:-1]
    inner = inner.at[:, :, -1].add(
        jnp.einsum("fh,rfwc->rhwc", hots[0], spread[:, :, 0, 1:-1], precision=highest)
    )
    inner = inner.at[:, :, :, 0].add(
        jnp.einsum("fh,rfwc->rhwc", hots[1], spread[:, :, 1:-1, -1], precision=highest)
    )
    inner = inner.at[:, :, 0].add(
        jnp.einsum("fh,rfwc->rhwc", hots[2], spread[:, :, -1, 1:-1], precision=highest)
    )
    inner = inner.at[:, :, :, -1].add(
        jnp.einsum("fh,rfwc->rhwc", hots[3], spread[:, :, 1:-1, 0], precision=highest)
    )
    return inner


def conv_apply(padded, weight):
    edge_len = padded.shape[2] - 2
    channels = weight.shape[1]
    taps_weight = weight.reshape(9, channels, channels)
    flat_padded = padded.reshape(-1, channels)
    products = jnp.einsum(
        "pc,tcd->ptd", flat_padded, taps_weight, preferred_element_type=jnp.float32
    )
    products = products.reshape(padded.shape[:4] + (9, channels))
    summed = None
    for tap_index, (row_off, col_off) in enumerate(tap_offsets):
        part = products[:, :, row_off : row_off + edge_len, col_off : col_off + edge_len, tap_index]
        summed = part if summed is None else summed + part
    return summed


def conv_back(padded, grad, weight):
    channels = weight.shape[1]
    taps_weight = weight.reshape(9, channels, channels)
    flat_grad = grad.reshape(-1, channels)
    pulled = jnp.einsum("pd,tcd->ptc", flat_grad, taps_weight, preferred_element_type=jnp.float32)
    pulled = pulled.reshape(grad.shape[:4] + (9, channels))
    spread = None
    placed = []
    for tap_index, (row_off, col_off) in enumerate(tap_offsets):
        widths = ((0, 0), (0, 0), (row_off, 2 - row_off), (col_off, 2 - col_off), (0, 0))
        moved = jnp.pad(pulled[:, :, :, :, tap_index], widths)
        spread = moved if spread is None else spread + moved
        placed.append(jnp.pad(grad, widths))
    stacked = jnp.stack(placed, axis=4).reshape(-1, 9, channels)
    flat_padded = padded.reshape(-1, channels)
    weight_grad = jnp.einsum(
        "pc,ptd->tcd", flat_padded, stacked, preferred_element_type=jnp.float32
    )
    return (weight_grad.reshape(9 * channels, channels), spread)


def gelu_tanh(v):
    return jax.nn.gelu(v, approximate=True)


def forward_pass(fields, hots_low, gathered):
    pad_in = pad_faces(fields, hots_low)
    pre_one = conv_apply(pad_in, gathered[0])
    hidden = gelu_tanh(pre_one).astype(jnp.bfloat16)
    pad_hidden = pad_faces(hidden, hots_low)
    pre_two = conv_apply(pad_hidden, gathered[1])
    return (pad_in, pre_one, pad_hidden, pre_two)


def adamw(weight, moment, square, grad, rate):
    moment_new = 0.9 * moment + 0.1 * grad
    square_new = 0.999 * square + 0.001 * grad * grad
    fix_one = 1.0 - 0.9**STEP_COUNT
    fix_two = 1.0 - 0.999**STEP_COUNT
    weight_new = weight - rate * (
        moment_new / fix_one / (jnp.sqrt(square_new / fix_two) + 1e-08) + 0.01 * weight
    )
    return (weight_new, moment_new, square_new)


def per_device(
    inputs,
    cotangent,
    lengths,
    face_table,
    w_first,
    w_second,
    w_skip,
    mom_first,
    sq_first,
    mom_second,
    sq_second,
    mom_skip,
    sq_skip,
):
    fields = inputs[0]
    channels = fields.shape[-1]
    hots_low = face_hots(face_table, jnp.bfloat16)
    hots_full = face_hots(face_table, jnp.float32)
    low_weights = (
        w_first.astype(jnp.bfloat16),
        w_second.astype(jnp.bfloat16),
        w_skip.astype(jnp.bfloat16),
    )
    gathered = (
        lax.all_gather(low_weights[0], "fsdp", axis=0, tiled=True),
        lax.all_gather(low_weights[1], "fsdp", axis=0, tiled=True),
        lax.all_gather(low_weights[2], "fsdp", axis=0, tiled=True),
    )
    saved = forward_pass(fields, hots_low, gathered)
    flat_fields = fields.reshape(-1, channels)
    skipped = jnp.dot(flat_fields, gathered[2], preferred_element_type=jnp.float32).reshape(
        fields.shape
    )
    output = (gelu_tanh(saved[3]) + skipped).astype(jnp.bfloat16)
    gathered = (
        lax.all_gather(low_weights[0], "fsdp", axis=0, tiled=True),
        lax.all_gather(low_weights[1], "fsdp", axis=0, tiled=True),
        lax.all_gather(low_weights[2], "fsdp", axis=0, tiled=True),
    )
    saved = forward_pass(fields, hots_low, gathered)
    pad_in, pre_one, pad_hidden, pre_two = saved
    live = (jnp.arange(fields.shape[0]) < lengths[0]).astype(jnp.bfloat16)
    grad_out = cotangent[0] * live[:, None, None, None, None]
    flat_out = grad_out.reshape(-1, channels)
    dw_skip = lax.dot_general(
        flat_fields, flat_out, (((0,), (0,)), ((), ())), preferred_element_type=jnp.float32
    )
    gelu_pull_two = jax.vjp(gelu_tanh, pre_two)[1]
    grad_two = gelu_pull_two(grad_out.astype(jnp.float32))[0].astype(jnp.bfloat16)
    dw_second, spread_hidden = conv_back(pad_hidden, grad_two, gathered[1])
    grad_hidden = unpad_back(spread_hidden, hots_full)
    gelu_pull_one = jax.vjp(gelu_tanh, pre_one)[1]
    grad_one = gelu_pull_one(grad_hidden)[0].astype(jnp.bfloat16)
    dw_first, spread_in = conv_back(pad_in, grad_one, gathered[0])
    skip_back = lax.dot_general(
        flat_out, gathered[2], (((1,), (1,)), ((), ())), preferred_element_type=jnp.float32
    )
    grad_inputs = unpad_back(spread_in, hots_full) + skip_back.reshape(fields.shape)
    shards = (
        lax.psum_scatter(
            dw_first.astype(jnp.bfloat16), "fsdp", scatter_dimension=0, tiled=True
        ).astype(jnp.float32),
        lax.psum_scatter(
            dw_second.astype(jnp.bfloat16), "fsdp", scatter_dimension=0, tiled=True
        ).astype(jnp.float32),
        lax.psum_scatter(
            dw_skip.astype(jnp.bfloat16), "fsdp", scatter_dimension=0, tiled=True
        ).astype(jnp.float32),
    )
    rate_conv = (9 * C) ** (-0.5)
    rate_skip = C ** (-0.5)
    totals = (
        lax.psum(shards[0].astype(jnp.bfloat16), "dp").astype(jnp.float32),
        lax.psum(shards[1].astype(jnp.bfloat16), "dp").astype(jnp.float32),
        lax.psum(shards[2].astype(jnp.bfloat16), "dp").astype(jnp.float32),
    )
    first_set = adamw(w_first, mom_first, sq_first, totals[0], rate_conv)
    second_set = adamw(w_second, mom_second, sq_second, totals[1], rate_conv)
    skip_set = adamw(w_skip, mom_skip, sq_skip, totals[2], rate_skip)
    return (
        output[None],
        grad_inputs[None],
        first_set[0],
        first_set[1],
        first_set[2],
        second_set[0],
        second_set[1],
        second_set[2],
        skip_set[0],
        skip_set[1],
        skip_set[2],
    )


def solution(mesh):
    placed = (
        P(("dp", "fsdp"), None, None, None, None, None),
        P(("dp", "fsdp"), None, None, None, None, None),
        P(("dp", "fsdp")),
        P(),
        P("fsdp", None),
        P("fsdp", None),
        P("fsdp", None),
        P("fsdp", None),
        P("fsdp", None),
        P("fsdp", None),
        P("fsdp", None),
        P("fsdp", None),
        P("fsdp", None),
    )
    return jax.shard_map(
        per_device,
        mesh=mesh,
        in_specs=placed,
        out_specs=(
            P(("dp", "fsdp"), None, None, None, None, None),
            P(("dp", "fsdp"), None, None, None, None, None),
            P("fsdp", None),
            P("fsdp", None),
            P("fsdp", None),
            P("fsdp", None),
            P("fsdp", None),
            P("fsdp", None),
            P("fsdp", None),
            P("fsdp", None),
            P("fsdp", None),
        ),
        check_vma=False,
    )
```

profile of v0, /device:TPU:0, one launch (start us, length us, event | category | flops | bytes accessed | tf_op | source)
XLA Modules:
  0.0 511.8 jit_solution(13693216425621798046)
XLA Ops:
  7.9 5.0 fusion.84
  15.4 2.5 copy.510
  22.2 2.4 maximum_bitcast_fusion
  24.7 11.0 %reduce-scatter.10.cloned.1.call-done = bf16[64,256]{1,0:T(8,128)(2,1)} async-done(((bf16[256,256]{1,0:T(8,128)(2,1)}), bf16[64,256]{1,0:T(8,128)(2,1)}) %reduce-scatter.10.cloned.1.call-update) | async-done | bytes 32784 | tf_op jit(solution)/shard_map/reduce_scatter | solution.py:182
  35.7 23.7 %psum.23 = bf16[64,256]{1,0:T(8,128)(2,1)S(1)} all-reduce(bf16[64,256]{1,0:T(8,128)(2,1)} %reduce-scatter.10.cloned.1.call-done), channel_id=1, replica_groups=mesh['dp'=8,'fsdp'=4] {'dp'}, use_global_device_ids=true, to_apply=%region_5.6 | all-reduce | flops 16384 | bytes 65536 | tf_op jit(solution)/shard_map/psum | solution.py:191
  60.2 14.7 %all_gather.14 = bf16[256,256]{1,0:T(8,128)(2,1)} all-gather(bf16[64,256]{1,0:T(8,128)(2,1)S(1)} %get-tuple-element.194), channel_id=1, replica_groups=mesh['dp'=8,'fsdp'=4] {'fsdp'}, dimensions={0}, use_global_device_ids=true | all-gather | bytes 163840 | tf_op jit(solution)/shard_map/all_gather | solution.py:143
  74.8 24.0 %fusion.33 = f32[8,12,8,8,9,256]{5,3,4,2,1,0:T(8,128)} fusion(bf16[9,256,256,1,1,1]{2,1,0,5,4,3:T(8,128)(2,1)} %bitcast.404, bf16[8,12,8,8,256,1]{4,1,3,0,2,5:T(8,128)(2,1)} %maximum_bitcast_fusion), kind=kOutput, calls=%fused_computation.102 | convolution fusion | flops 7247757312 | bytes 60948480 | tf_op jit(solution)/shard_map/pc,tcd->ptd/dot_general | solution.py:60
  98.8 17.8 %multiply_convert_fusion = (bf16[8,12,6,6,256]{4,3,2,1,0:T(8,128)(2,1)S(1)}, f32[8,12,6,6,256]{4,3,2,1,0:T(8,128)}) fusion(f32[8,12,8,8,9,256]{5,3,4,2,1,0:T(8,128)} %fusion.33), kind=kLoop, calls=%fused_computation.78 | loop fusion | flops 15040512 | bytes 37158912 | tf_op jit(solution)/shard_map/convert_element_type | solution.py:99
  123.0 22.2 %fusion.115 = f32[8,12,8,8,9,256]{5,3,2,1,0,4:T(8,128)} fusion(bf16[9,256,256,1,1,1]{2,1,5,4,3,0:T(8,128)(2,1)} %bitcast.402, bf16[8,12,1,8,256]{4,3,2,1,0:T(8,128)(2,1)} %copy.301, bf16[8,12,6,1,256]{4,3,2,1,0:T(2,128)(2,1)S(1)} %copy.296, bf16[8,12,6,6,256]{4,3,2,1,0:T(8,128)(2,1)S(1)} %get-tuple-element.164, bf16[8,12,6,1,256]{4,3,2,1,0:T(2,128)(2,1)S(1)} %copy.295, ...), kind=kOutput, calls=%fused_computation.210 | convolution fusion | flops 7263485952 | bytes 60948480 | tf_op jit(solution)/shard_map/pc,tcd->ptd/dot_general | solution.py:60
  145.3 18.2 %fusion.7 = (bf16[8,12,6,6,256]{4,3,2,1,0:T(8,128)(2,1)S(1)}, f32[8,12,6,6,1,256]{5,3,2,1,0,4:T(8,128)}) fusion(bf16[8]{0:T(256)(128)(2,1)S(1)} %copy-done.29, bf16[1,8,12,6,6,256]{5,1,4,3,2,0:T(8,128)(2,1)S(1)} %copy-done.1, f32[8,12,8,8,9,256]{5,3,2,1,0,4:T(8,128)} %fusion.115), kind=kLoop, calls=%fused_computation.19 | loop fusion | flops 26542080 | bytes 38928400 | tf_op jit(solution)/shard_map/convert_element_type | solution.py:165
  163.5 19.7 %fusion.40 = f32[8,12,6,6,9,256]{5,3,2,1,0,4:T(8,128)} fusion(bf16[9,256,256,1,1,1]{2,1,5,4,3,0:T(8,128)(2,1)S(1)} %bitcast.403, f32[8,12,6,6,1,256]{5,3,2,1,0,4:T(8,128)} %get-tuple-element.163, bf16[1,8,12,6,6,256]{5,1,4,3,2,0:T(8,128)(2,1)} %param.30, bf16[8]{0:T(256)(128)(2,1)} %copy-done.28), kind=kOutput, calls=%fused_computation.113 | convolution fusion | flops 4098097152 | bytes 38338576 | tf_op jit(solution)/shard_map/pd,tcd->ptc/dot_general | solution.py:75
  183.2 30.6 %slice_bitcast_fusion.17 = (f32[8,12,6,6,256]{4,3,2,1,0:T(8,128)}, f32[8,12,6,6,256]{4,3,2,1,0:T(8,128)}, f32[8,12,6,6,256]{4,3,2,1,0:T(8,128)}, f32[8,12,6,6,25...) fusion(f32[8,12,6,6,9,256]{5,3,2,1,0,4:T(8,128)} %fusion.40), kind=kLoop, calls=%fused_computation.56 | loop fusion | bytes 63700992 | tf_op jit(solution)/shard_map/squeeze | solution.py:81
  213.8 18.5 %pad_add_fusion.1 = f32[8,12,8,8,256]{4,3,2,1,0:T(8,128)} fusion(f32[8,12,6,6,256]{4,3,2,1,0:T(8,128)} %get-tuple-element.183, f32[8,12,6,6,256]{4,3,2,1,0:T(8,128)} %get-tuple-element.176, f32[8,12,6,6,256]{4,3,2,1,0:T(8,128)} %get-tuple-element.177, f32[8,12,6,6,256]{4,3,2,1,0:T(8,128)} %get-tuple-element.178, f32[8,12,6,6,256]{4,3,2,1,0:T(8,128)} %get-tuple-element.179, ...), kind=kLoop, calls=%fused_computation.7 | loop fusion | flops 12582912 | bytes 38141952 | tf_op jit(solution)/shard_map/add | solution.py:82
  232.3 4.9 fusion.175
  237.2 2.7 slice_bitcast_fusion.26
  239.9 5.3 %slice.563 = f32[8,12,6,6,256]{4,3,2,1,0:T(8,128)} slice(f32[8,12,8,8,256]{4,3,2,1,0:T(8,128)} %pad_add_fusion.1), slice={[0:8], [0:12], [1:7], [1:7], [0:256]} | slice | bytes 7077888 | tf_op jit(solution)/shard_map/slice | solution.py:39
  247.5 2.5 bitcast_dynamic-update-slice_fusion.7
  249.9 2.5 bitcast_dynamic-update-slice_fusion.6
  257.2 2.4 bitcast_dynamic-update-slice_fusion.3
  262.1 2.5 bitcast_dynamic-update-slice_fusion.1
  267.0 13.9 %bitcast_convert_fusion = bf16[9,256,256]{1,2,0:T(8,128)(2,1)} fusion(bf16[8,12,8,8,9,256]{5,3,2,1,0,4:T(8,128)(2,1)} %bitcast_dynamic-update-slice_fusion, bf16[8,12,1,8,256]{4,3,2,1,0:T(8,128)(2,1)S(1)} %copy-done.19, bf16[8,12,6,1,256]{4,3,2,1,0:T(2,128)(2,1)S(1)} %copy-done.16, bf16[8,12,6,6,256]{4,3,2,1,0:T(8,128)(2,1)S(1)} %copy-done.3, ...), kind=kOutput, calls=%fused_computation.111 | convolution fusion | flops 7264075776 | bytes 32636928 | tf_op jit(solution)/shard_map/pc,ptd->tcd/dot_general | solution.py:86
  283.8 2.6 fusion.90
  286.4 3.2 slice_add_fusion.19
  289.6 13.0 %scatter-add.29 = f32[8,12,6,6,256]{4,3,2,1,0:T(8,128)} dynamic-update-slice(f32[8,12,6,6,256]{4,3,2,1,0:T(8,128)} %fusion.90, f32[8,12,6,1,256]{4,3,2,1,0:T(1,128)S(1)} %slice_add_fusion.19, s32[]{:T(128)} %constant.226.clone.1, s32[]{:T(128)} %constant.226.clone.1, s32[]{:T(128)} %constant.226.clone.1, s32[]{:T(128)} %constant.226.clone.1, s32[]{:T(128)} %constant.226.clone.1) | dynamic-update-slice | bytes 1179652 | tf_op jit(solution)/shard_map/scatter-add | solution.py:43
  302.6 2.5 fusion.89
  305.1 3.4 slice_add_fusion.18
  308.5 13.0 %scatter-add.31 = f32[8,12,6,6,256]{4,3,2,1,0:T(8,128)} dynamic-update-slice(f32[8,12,6,6,256]{4,3,2,1,0:T(8,128)} %fusion.89, f32[8,12,6,1,256]{4,3,2,1,0:T(1,128)S(1)} %slice_add_fusion.18, s32[]{:T(128)} %constant.226.clone.1, s32[]{:T(128)} %constant.226.clone.1, s32[]{:T(128)} %constant.226.clone.1, s32[]{:T(128)} %constant.227.clone.1, s32[]{:T(128)} %constant.226.clone.1) | dynamic-update-slice | bytes 1179652 | tf_op jit(solution)/shard_map/scatter-add | solution.py:49
  321.5 5.5 %fusion.16 = bf16[8,12,6,6,256]{4,3,2,1,0:T(8,128)(2,1)S(1)} fusion(f32[8,12,6,6,256]{4,3,2,1,0:T(8,128)} %get-tuple-element.165, f32[8,12,6,6,256]{4,3,2,1,0:T(8,128)} %scatter-add.31), kind=kLoop, calls=%fused_computation.28 | loop fusion | flops 17694720 | bytes 8847360 | tf_op jit(solution)/shard_map/convert_element_type | solution.py:169
  329.3 2.4 bitcast_dynamic-update-slice_fusion.16
  336.5 2.4 bitcast_dynamic-update-slice_fusion.13
  338.9 2.4 bitcast_dynamic-update-slice_fusion.12
  343.8 2.4 bitcast_dynamic-update-slice_fusion.10
  346.2 2.5 bitcast_dynamic-update-slice_fusion.9
  348.7 16.7 %fusion.43 = f32[8,12,6,6,9,256]{5,1,4,3,2,0:T(8,128)} fusion(bf16[9,256,256,1,1,1]{2,1,0,5,4,3:T(8,128)(2,1)S(1)} %bitcast.405, bf16[8,12,6,6,256,1]{4,3,2,1,0,5:T(8,128)(2,1)S(1)} %bitcast.397), kind=kOutput, calls=%fused_computation.116 | convolution fusion | flops 4076863488 | bytes 34799616 | tf_op jit(solution)/shard_map/pd,tcd->ptc/dot_general | solution.py:75
  365.3 31.7 %slice_bitcast_fusion.8 = (f32[8,12,6,6,256]{4,1,3,2,0:T(8,128)}, f32[8,12,6,6,256]{4,1,3,2,0:T(8,128)}, f32[8,12,6,6,256]{4,1,3,2,0:T(8,128)}, f32[8,12,6,6,256...) fusion(f32[8,12,6,6,9,256]{5,1,4,3,2,0:T(8,128)} %fusion.43), kind=kLoop, calls=%fused_computation.47 | loop fusion | bytes 63700992 | tf_op jit(solution)/shard_map/squeeze | solution.py:81
  397.0 15.3 %bitcast_convert_fusion.1 = bf16[9,256,256]{1,2,0:T(8,128)(2,1)} fusion(bf16[8,12,8,8,9,256]{5,3,2,1,0,4:T(8,128)(2,1)} %bitcast_dynamic-update-slice_fusion.9, bf16[8,12,8,8,256,1]{4,1,3,0,2,5:T(8,128)(2,1)} %maximum_bitcast_fusion), kind=kOutput, calls=%fused_computation.112 | convolution fusion | flops 7248347136 | bytes 32636928 | tf_op jit(solution)/shard_map/pc,ptd->tcd/dot_general | solution.py:86
  412.4 4.9 fusion.53
  417.3 3.1 copy.352
  420.4 14.8 %pad_add_fusion = f32[8,12,8,8,256]{4,1,3,2,0:T(8,128)S(1)} fusion(f32[8,12,6,6,256]{4,1,3,2,0:T(8,128)} %get-tuple-element.173, f32[8,12,6,6,256]{4,1,3,2,0:T(8,128)} %get-tuple-element.174, f32[8,12,6,6,256]{4,1,3,2,0:T(8,128)} %get-tuple-element.167, f32[8,12,6,6,256]{4,1,3,2,0:T(8,128)} %get-tuple-element.168, f32[8,12,6,6,256]{4,1,3,2,0:T(8,128)} %get-tuple-element.169, ...), kind=kLoop, calls=%fused_computation | loop fusion | flops 12582912 | bytes 38141952 | tf_op jit(solution)/shard_map/add | solution.py:82
  435.3 2.7 slice.581
  439.4 2.6 fusion.63
  442.0 2.5 fusion.65
  444.5 2.5 fusion.67
  447.1 3.3 add_bitcast_fusion
  450.4 3.8 copy.353
  454.3 45.6 %all-reduce.43.cloned.1.call-done = (bf16[576,256]{1,0:T(8,128)(2,1)}, bf16[576,256]{1,0:T(8,128)(2,1)}) async-done(((bf16[576,256]{1,0:T(8,128)(2,1)}, bf16[576,256]{1,0:T(8,128)(2,1)}), (bf16[576,256]{1,0:T(8,128)(2,1)}, bf16[576,256]{1,0:T(8,128)(2,1)})) %all-reduce.43.cloned.1.call-update) | async-done | bytes 589840 | tf_op jit(solution)/shard_map/psum | solution.py:189
  499.8 2.4 multiply_subtract_fusion.1
  502.3 2.4 multiply_subtract_fusion
  (123 shorter events, 39.3 us)
Async XLA Ops:
  7.2 28.6 %reduce-scatter.10.cloned.1.call-start = ((), (), s32[]{:S(2)}) async-start(), calls=%async_computation.7 | async-start | bytes 163840 | tf_op jit(solution)/shard_map/reduce_scatter | solution.py:182
  7.9 10.1 %copy-start.28 = (bf16[8]{0:T(256)(128)(2,1)}, bf16[8]{0:T(256)(128)(2,1)S(1)}, u32[]{:S(2)}) copy-start(bf16[8]{0:T(256)(128)(2,1)S(1)} %compare_convert_fusion) | copy-start | bytes 52
  7.9 5.9 %copy-start.9 = (f32[576,256]{1,0:T(8,128)S(1)}, f32[576,256]{1,0:T(8,128)}, u32[]{:S(2)}) copy-start(f32[576,256]{1,0:T(8,128)} %param.33) | copy-start | bytes 1769476
  7.9 6.7 %copy-start.11 = (f32[576,256]{1,0:T(8,128)S(1)}, f32[576,256]{1,0:T(8,128)}, u32[]{:S(2)}) copy-start(f32[576,256]{1,0:T(8,128)} %param.34) | copy-start | bytes 1769476
  12.9 5.1 copy-start
  13.7 61.1 %all-gather.3.cloned.1.call-start = ((), (), s32[]{:S(2)}) async-start(), calls=%async_computation.3 | async-start | bytes 1474560 | tf_op jit(solution)/shard_map/all_gather | solution.py:141
  14.5 5.6 %copy-start.30 = (s32[12,4]{0,1:T(4,128)S(1)}, s32[12,4]{0,1:T(4,128)}, u32[]{:S(2)}) copy-start(s32[12,4]{0,1:T(4,128)} %param.32) | copy-start | bytes 580
  14.5 107.7 %all-gather.5.cloned.1.call-start = ((), (), s32[]{:S(2)}) async-start(), calls=%async_computation.4 | async-start | bytes 1474560 | tf_op jit(solution)/shard_map/all_gather | solution.py:142
  15.4 431.7 %reduce-scatter.8.cloned.1.call-start = ((), (), s32[]{:S(2)}) async-start(), calls=%async_computation.6 | async-start | bytes 1474560 | tf_op jit(solution)/shard_map/reduce_scatter | solution.py:179
  22.1 37.4 %copy-start.25 = (f32[64,256]{1,0:T(8,128)S(1)}, f32[64,256]{1,0:T(8,128)}, u32[]{:S(2)}) copy-start(f32[64,256]{1,0:T(8,128)} %param.35) | copy-start | bytes 196612
  22.1 37.4 %copy-start.26 = (f32[64,256]{1,0:T(8,128)S(1)}, f32[64,256]{1,0:T(8,128)}, u32[]{:S(2)}) copy-start(f32[64,256]{1,0:T(8,128)} %param.40) | copy-start | bytes 196612
  22.1 37.4 %copy-start.27 = (f32[64,256]{1,0:T(8,128)S(1)}, f32[64,256]{1,0:T(8,128)}, u32[]{:S(2)}) copy-start(f32[64,256]{1,0:T(8,128)} %param.41) | copy-start | bytes 196612
  116.6 5.7 %copy-start.2 = (bf16[8,12,6,6,256]{4,3,2,1,0:T(8,128)(2,1)}, bf16[8,12,6,6,256]{4,3,2,1,0:T(8,128)(2,1)S(1)}, u32[]{:S(2)}) copy-start(bf16[8,12,6,6,256]{4,3,2,1,0:T(8,128)(2,1)S(1)} %get-tuple-element.164) | copy-start | bytes 5308420
  121.4 0.9 copy-start.13
  122.2 0.8 copy-start.15
  123.0 22.3 %copy-start.1 = (bf16[1,8,12,6,6,256]{5,1,4,3,2,0:T(8,128)(2,1)S(1)}, bf16[1,8,12,6,6,256]{5,1,4,3,2,0:T(8,128)(2,1)}, u32[]{:S(2)}) copy-start(bf16[1,8,12,6,6,256]{5,1,4,3,2,0:T(8,128)(2,1)} %param.30) | copy-start | bytes 5308420
  123.0 22.3 %copy-start.29 = (bf16[8]{0:T(256)(128)(2,1)S(1)}, bf16[8]{0:T(256)(128)(2,1)}, u32[]{:S(2)}) copy-start(bf16[8]{0:T(256)(128)(2,1)} %copy-done.28) | copy-start | bytes 52
  145.3 18.2 %copy-start.5 = (bf16[2304,256]{1,0:T(8,128)(2,1)S(1)}, bf16[2304,256]{1,0:T(8,128)(2,1)}, u32[]{:S(2)}) copy-start(bf16[2304,256]{1,0:T(8,128)(2,1)} %all-gather.5.cloned.1.call-done) | copy-start | bytes 3538948
  262.0 4.9 copy-start.3
  262.0 4.9 copy-start.14
  262.0 4.9 copy-start.16
  262.0 4.9 copy-start.18
  262.0 4.9 copy-start.19
  280.9 1.5 copy-start.8
  280.9 2.2 copy-start.7
  280.9 166.2 %reduce-scatter.6.cloned.1.call-start = ((), (), s32[]{:S(2)}) async-start(), calls=%async_computation.5 | async-start | bytes 1474560 | tf_op jit(solution)/shard_map/reduce_scatter | solution.py:176
  343.8 4.9 copy-start.6
  397.0 15.4 %copy-start.17 = (bf16[1,8,12,6,6,256]{5,1,4,3,2,0:T(8,128)(2,1)S(1)}, bf16[1,8,12,6,6,256]{5,1,4,3,2,0:T(8,128)(2,1)}, u32[]{:S(2)}) copy-start(bf16[1,8,12,6,6,256]{5,1,4,3,2,0:T(8,128)(2,1)} %param.29) | copy-start | bytes 5308420
  397.0 15.4 %copy-start.24 = (bf16[256,256]{1,0:T(8,128)(2,1)S(1)}, bf16[256,256]{1,0:T(8,128)(2,1)}, u32[]{:S(2)}) copy-start(bf16[256,256]{1,0:T(8,128)(2,1)} %all_gather.14) | copy-start | bytes 393220
  412.4 87.5 %all-reduce.43.cloned.1.call-start = ((), (), s32[]{:S(2)}) async-start(), calls=%async_computation.8 | async-start | bytes 1179648 | tf_op jit(solution)/shard_map/psum | solution.py:189
  438.0 9.1 %copy-start.4 = (bf16[8,12,6,6,256]{4,3,2,1,0:T(8,128)(2,1)S(1)}, bf16[8,12,6,6,256]{4,3,2,1,0:T(8,128)(2,1)}, u32[]{:S(2)}) copy-start(bf16[8,12,6,6,256]{4,3,2,1,0:T(8,128)(2,1)} %fusion.39) | copy-start | bytes 5308420
  450.4 49.5 %copy-start.10 = (f32[576,256]{1,0:T(8,128)S(1)}, f32[576,256]{1,0:T(8,128)}, u32[]{:S(2)}) copy-start(f32[576,256]{1,0:T(8,128)} %param.33) | copy-start | bytes 1769476
  450.4 49.5 %copy-start.20 = (f32[576,256]{1,0:T(8,128)S(1)}, f32[576,256]{1,0:T(8,128)}, u32[]{:S(2)}) copy-start(f32[576,256]{1,0:T(8,128)} %param.36) | copy-start | bytes 1769476
  450.4 49.5 %copy-start.21 = (f32[576,256]{1,0:T(8,128)S(1)}, f32[576,256]{1,0:T(8,128)}, u32[]{:S(2)}) copy-start(f32[576,256]{1,0:T(8,128)} %param.37) | copy-start | bytes 1769476
  450.4 51.9 %copy-start.12 = (f32[576,256]{1,0:T(8,128)S(1)}, f32[576,256]{1,0:T(8,128)}, u32[]{:S(2)}) copy-start(f32[576,256]{1,0:T(8,128)} %param.34) | copy-start | bytes 1769476
  450.4 51.9 %copy-start.22 = (f32[576,256]{1,0:T(8,128)S(1)}, f32[576,256]{1,0:T(8,128)}, u32[]{:S(2)}) copy-start(f32[576,256]{1,0:T(8,128)} %param.38) | copy-start | bytes 1769476
  450.4 51.9 %copy-start.23 = (f32[576,256]{1,0:T(8,128)S(1)}, f32[576,256]{1,0:T(8,128)}, u32[]{:S(2)}) copy-start(f32[576,256]{1,0:T(8,128)} %param.39) | copy-start | bytes 1769476
Sparse Core Ops, SparseCore 0:
  13.8 21.8 reduce-scatter.9
  38.0 30.0 all-gather.2
  70.2 29.5 all-gather.4
  281.0 26.5 reduce-scatter.7
  412.5 26.7 reduce-scatter.5
  447.2 52.5 all-reduce.42
where the time goes:
time: 519 us; the launch traced here: 512 us
  local copies, waits for them, and re-layouts  163 us (31%)
  matrix products  139 us (27%)
  other arithmetic  98.3 us (19%)
  waiting for transfers between devices  56.7 us (11%)
  blocking collectives  38.4 us (7%)
  between operations  15.6 us (3%)
    squeeze x2, local copies, waits for them, and re-layouts, conv_back(): moved = jnp.pad(pulled[:, :, :, :, tap_index], widths)  62.2 us
    unnamed x82, local copies, waits for them, and re-layouts  49.7 us
    dot_general x2, matrix products, conv_apply(): jnp.einsum('pc,tcd->ptd', flat_padded, taps_weight, preferred_element_typ...  46.2 us
    psum x1, waiting for transfers between devices, per_device(): lax.psum(shards[0].astype(jnp.bfloat16), 'dp').astype(jnp.float32)  45.6 us
    dot_general x2, matrix products, conv_back(): jnp.einsum('pd,tcd->ptc', flat_grad, taps_weight, preferred_element_type=...  36.3 us
    add x2, other arithmetic, conv_back(): spread = moved if spread is None else spread + moved  33.3 us
    dot_general x2, matrix products, conv_back(): jnp.einsum('pc,ptd->tcd', flat_padded, stacked, preferred_element_type=jn...  29.2 us
    psum x1, blocking collectives, per_device(): lax.psum(shards[2].astype(jnp.bfloat16), 'dp').astype(jnp.float32)  23.7 us
  transfers between devices with their start and end apart: 6, of which 2 were waited for; matrix products, arithmetic and copies ran while one was open for 45% of the time, Pallas kernels for 0%

commit v1 on v0

--- a/solution.py
+++ b/solution.py
@@ -6,6 +6,28 @@
 C = 256
 STEP_COUNT = 10
 tap_offsets = [(row_off, col_off) for row_off in range(3) for col_off in range(3)]
+
+
+def laid_out(blocks, dim):
+    blocks = jnp.moveaxis(blocks, 0, dim)
+    lengths = blocks.shape
+    return blocks.reshape(*lengths[:dim], lengths[dim] * lengths[dim + 1], *lengths[dim + 2 :])
+
+
+def doubled(shard, axis):
+    size = lax.axis_size(axis)
+    blocks = shard[None]
+    for level in range(size.bit_length() - 1):
+        distance = 1 << level
+        partner_block = lax.ppermute(blocks, axis, [(i, i ^ distance) for i in range(size)])
+        both = jnp.stack([blocks, partner_block])
+        upper = lax.axis_index(axis) >> level & 1
+        blocks = jnp.where(upper == 0, both, both[::-1]).reshape(-1, *shard.shape)
+    return blocks
+
+
+def collect(x, axis, dim):
+    return laid_out(doubled(x, axis), dim)
 
 
 def face_hots(face_table, dtype):
@@ -140,7 +162,7 @@
     gathered = (
         lax.all_gather(low_weights[0], "fsdp", axis=0, tiled=True),
         lax.all_gather(low_weights[1], "fsdp", axis=0, tiled=True),
-        lax.all_gather(low_weights[2], "fsdp", axis=0, tiled=True),
+        collect(low_weights[2], "fsdp", 0),
     )
     saved = forward_pass(fields, hots_low, gathered)
     flat_fields = fields.reshape(-1, channels)

time: 519 us -> 544 us (1.048)
  local copies, waits for them, and re-layouts: 163 us -> 175 us
  waiting for transfers between devices: 56.7 us -> 65.3 us
  other arithmetic: 98.3 us -> 105 us
    unnamed x82 -> x85, local copies, waits for them, and re-layouts: 49.7 us -> 50.2 us
  transfers between devices with their start and end apart: 6 -> 8, of which waited for: 2 -> 3; matrix products, arithmetic and copies ran while one was open for 45% -> 46% of each run, Pallas kernels for 0% -> 0%
where the time goes in v1:
time: 544 us; the launch traced here: 536 us
  local copies, waits for them, and re-layouts  175 us (32%)
  matrix products  136 us (25%)
  other arithmetic  105 us (19%)
  waiting for transfers between devices  65.3 us (12%)
  blocking collectives  39.3 us (7%)
  between operations  15.6 us (3%)
    squeeze x2, local copies, waits for them, and re-layouts, conv_back(): moved = jnp.pad(pulled[:, :, :, :, tap_index], widths)  62.2 us
    unnamed x85, local copies, waits for them, and re-layouts  50.2 us
    psum x1, waiting for transfers between devices, per_device(): lax.psum(shards[0].astype(jnp.bfloat16), 'dp').astype(jnp.float32)  46.8 us
    dot_general x2, matrix products, conv_apply(): jnp.einsum('pc,tcd->ptd', flat_padded, taps_weight, preferred_element_typ...  45.9 us
    dot_general x2, matrix products, conv_back(): jnp.einsum('pd,tcd->ptc', flat_grad, taps_weight, preferred_element_type=...  36.3 us
    add x2, other arithmetic, conv_back(): spread = moved if spread is None else spread + moved  33.5 us
    dot_general x2, matrix products, conv_back(): jnp.einsum('pc,ptd->tcd', flat_padded, stacked, preferred_element_type=jn...  29.2 us
    psum x1, blocking collectives, per_device(): lax.psum(shards[2].astype(jnp.bfloat16), 'dp').astype(jnp.float32)  23.7 us
  transfers between devices with their start and end apart: 8, of which 3 were waited for; matrix products, arithmetic and copies ran while one was open for 46% of the time, Pallas kernels for 0%

profile of v1, /device:TPU:0, one launch (start us, length us, event | category | flops | bytes accessed | tf_op | source)
XLA Modules:
  0.0 536.0 jit_solution(16305828818428210135)
XLA Ops:
  7.9 5.0 fusion.79
  19.4 16.4 %reduce-scatter.10.cloned.1.call-done = bf16[64,256]{1,0:T(8,128)(2,1)} async-done(((bf16[256,256]{1,0:T(8,128)(2,1)}), bf16[64,256]{1,0:T(8,128)(2,1)}) %reduce-scatter.10.cloned.1.call-update) | async-done | bytes 32784 | tf_op jit(solution)/shard_map/reduce_scatter | solution.py:204
  35.8 23.7 %psum.23 = bf16[64,256]{1,0:T(8,128)(2,1)S(1)} all-reduce(bf16[64,256]{1,0:T(8,128)(2,1)} %reduce-scatter.10.cloned.1.call-done), channel_id=1, replica_groups=mesh['dp'=8,'fsdp'=4] {'dp'}, use_global_device_ids=true, to_apply=%region_5.6 | all-reduce | flops 16384 | bytes 65536 | tf_op jit(solution)/shard_map/psum | solution.py:213
  60.2 3.8 maximum_bitcast_fusion
  72.3 15.6 %all_gather.13 = bf16[256,256]{1,0:T(8,128)(2,1)} all-gather(bf16[64,256]{1,0:T(8,128)(2,1)S(1)} %get-tuple-element.194), channel_id=1, replica_groups=mesh['dp'=8,'fsdp'=4] {'fsdp'}, dimensions={0}, use_global_device_ids=true | all-gather | bytes 163840 | tf_op jit(solution)/shard_map/all_gather | solution.py:176
  90.1 2.9 copy.311
  93.1 4.8 reshape.705
  97.9 23.2 %fusion.33 = f32[8,12,8,8,9,256]{5,3,4,2,1,0:T(8,128)} fusion(bf16[9,256,256,1,1,1]{2,1,0,5,4,3:T(8,128)(2,1)} %bitcast.411, bf16[8,12,8,8,256,1]{4,1,3,0,2,5:T(8,128)(2,1)} %maximum_bitcast_fusion), kind=kOutput, calls=%fused_computation.103 | convolution fusion | flops 7247757312 | bytes 60948480 | tf_op jit(solution)/shard_map/pc,tcd->ptd/dot_general | solution.py:82
  121.1 17.8 %multiply_convert_fusion = (bf16[8,12,6,6,256]{4,3,2,1,0:T(8,128)(2,1)S(1)}, f32[8,12,6,6,256]{4,3,2,1,0:T(8,128)}) fusion(f32[8,12,8,8,9,256]{5,3,4,2,1,0:T(8,128)} %fusion.33), kind=kLoop, calls=%fused_computation.79 | loop fusion | flops 15040512 | bytes 37158912 | tf_op jit(solution)/shard_map/convert_element_type | solution.py:121
  145.2 22.7 %fusion.110 = f32[8,12,8,8,9,256]{5,3,2,1,0,4:T(8,128)} fusion(bf16[9,256,256,1,1,1]{2,1,5,4,3,0:T(8,128)(2,1)} %bitcast.409, bf16[8,12,1,8,256]{4,3,2,1,0:T(8,128)(2,1)} %copy.300, bf16[8,12,6,1,256]{4,3,2,1,0:T(2,128)(2,1)S(1)} %copy.295, bf16[8,12,6,6,256]{4,3,2,1,0:T(8,128)(2,1)S(1)} %get-tuple-element.164, bf16[8,12,6,1,256]{4,3,2,1,0:T(2,128)(2,1)S(1)} %copy.294, ...), kind=kOutput, calls=%fused_computation.208 | convolution fusion | flops 7263485952 | bytes 60948480 | tf_op jit(solution)/shard_map/pc,tcd->ptd/dot_general | solution.py:82
  167.9 18.1 %fusion.7 = (bf16[8,12,6,6,256]{4,3,2,1,0:T(8,128)(2,1)S(1)}, f32[8,12,6,6,1,256]{5,3,2,1,0,4:T(8,128)}) fusion(bf16[8]{0:T(256)(128)(2,1)S(1)} %copy-done.30, bf16[1,8,12,6,6,256]{5,1,4,3,2,0:T(8,128)(2,1)S(1)} %copy-done.1, f32[8,12,8,8,9,256]{5,3,2,1,0,4:T(8,128)} %fusion.110), kind=kLoop, calls=%fused_computation.20 | loop fusion | flops 26542080 | bytes 38928400 | tf_op jit(solution)/shard_map/convert_element_type | solution.py:187
  186.0 19.7 %fusion.36 = f32[8,12,6,6,9,256]{5,3,2,1,0,4:T(8,128)} fusion(bf16[9,256,256,1,1,1]{2,1,5,4,3,0:T(8,128)(2,1)S(1)} %bitcast.410, f32[8,12,6,6,1,256]{5,3,2,1,0,4:T(8,128)} %get-tuple-element.163, bf16[1,8,12,6,6,256]{5,1,4,3,2,0:T(8,128)(2,1)} %param.30, bf16[8]{0:T(256)(128)(2,1)} %copy-done.29), kind=kOutput, calls=%fused_computation.110 | convolution fusion | flops 4098097152 | bytes 38338576 | tf_op jit(solution)/shard_map/pd,tcd->ptc/dot_general | solution.py:97
  205.7 30.6 %slice_bitcast_fusion.17 = (f32[8,12,6,6,256]{4,3,2,1,0:T(8,128)}, f32[8,12,6,6,256]{4,3,2,1,0:T(8,128)}, f32[8,12,6,6,256]{4,3,2,1,0:T(8,128)}, f32[8,12,6,6,25...) fusion(f32[8,12,6,6,9,256]{5,3,2,1,0,4:T(8,128)} %fusion.36), kind=kLoop, calls=%fused_computation.57 | loop fusion | bytes 63700992 | tf_op jit(solution)/shard_map/squeeze | solution.py:103
  236.3 18.5 %pad_add_fusion.1 = f32[8,12,8,8,256]{4,3,2,1,0:T(8,128)} fusion(f32[8,12,6,6,256]{4,3,2,1,0:T(8,128)} %get-tuple-element.183, f32[8,12,6,6,256]{4,3,2,1,0:T(8,128)} %get-tuple-element.176, f32[8,12,6,6,256]{4,3,2,1,0:T(8,128)} %get-tuple-element.177, f32[8,12,6,6,256]{4,3,2,1,0:T(8,128)} %get-tuple-element.178, f32[8,12,6,6,256]{4,3,2,1,0:T(8,128)} %get-tuple-element.179, ...), kind=kLoop, calls=%fused_computation.7 | loop fusion | flops 12582912 | bytes 38141952 | tf_op jit(solution)/shard_map/add | solution.py:104
  254.8 4.9 fusion.171
  259.7 2.7 slice_bitcast_fusion.26
  262.4 5.3 slice.563
  270.0 2.5 bitcast_dynamic-update-slice_fusion.7
  272.4 2.5 bitcast_dynamic-update-slice_fusion.6
  279.7 2.4 bitcast_dynamic-update-slice_fusion.3
  284.5 2.5 bitcast_dynamic-update-slice_fusion.1
  289.4 13.9 %bitcast_convert_fusion = bf16[9,256,256]{1,2,0:T(8,128)(2,1)} fusion(bf16[8,12,8,8,9,256]{5,3,2,1,0,4:T(8,128)(2,1)} %bitcast_dynamic-update-slice_fusion, bf16[8,12,1,8,256]{4,3,2,1,0:T(8,128)(2,1)S(1)} %copy-done.20, bf16[8,12,6,1,256]{4,3,2,1,0:T(2,128)(2,1)S(1)} %copy-done.18, bf16[8,12,6,6,256]{4,3,2,1,0:T(8,128)(2,1)S(1)} %copy-done.3, ...), kind=kOutput, calls=%fused_computation.108 | convolution fusion | flops 7264075776 | bytes 32636928 | tf_op jit(solution)/shard_map/pc,ptd->tcd/dot_general | solution.py:108
  305.9 2.5 fusion.85
  308.4 3.2 slice_add_fusion.19
  311.7 13.4 %scatter-add.29 = f32[8,12,6,6,256]{4,3,2,1,0:T(8,128)} dynamic-update-slice(f32[8,12,6,6,256]{4,3,2,1,0:T(8,128)} %fusion.85, f32[8,12,6,1,256]{4,3,2,1,0:T(1,128)S(1)} %slice_add_fusion.19, s32[]{:T(128)} %constant.229.clone.1, s32[]{:T(128)} %constant.229.clone.1, s32[]{:T(128)} %constant.229.clone.1, s32[]{:T(128)} %constant.229.clone.1, s32[]{:T(128)} %constant.229.clone.1) | dynamic-update-slice | bytes 1179652 | tf_op jit(solution)/shard_map/scatter-add | solution.py:65
  325.0 2.5 fusion.84
  327.5 3.4 slice_add_fusion.18
  330.9 13.0 %scatter-add.31 = f32[8,12,6,6,256]{4,3,2,1,0:T(8,128)} dynamic-update-slice(f32[8,12,6,6,256]{4,3,2,1,0:T(8,128)} %fusion.84, f32[8,12,6,1,256]{4,3,2,1,0:T(1,128)S(1)} %slice_add_fusion.18, s32[]{:T(128)} %constant.229.clone.1, s32[]{:T(128)} %constant.229.clone.1, s32[]{:T(128)} %constant.229.clone.1, s32[]{:T(128)} %constant.233.clone.1, s32[]{:T(128)} %constant.229.clone.1) | dynamic-update-slice | bytes 1179652 | tf_op jit(solution)/shard_map/scatter-add | solution.py:71
  343.9 5.5 %fusion.16 = bf16[8,12,6,6,256]{4,3,2,1,0:T(8,128)(2,1)S(1)} fusion(f32[8,12,6,6,256]{4,3,2,1,0:T(8,128)} %get-tuple-element.165, f32[8,12,6,6,256]{4,3,2,1,0:T(8,128)} %scatter-add.31), kind=kLoop, calls=%fused_computation.29 | loop fusion | flops 17694720 | bytes 8847360 | tf_op jit(solution)/shard_map/convert_element_type | solution.py:191
  351.7 2.4 bitcast_dynamic-update-slice_fusion.16
  358.9 2.5 bitcast_dynamic-update-slice_fusion.13
  361.3 2.5 bitcast_dynamic-update-slice_fusion.12
  368.6 2.5 bitcast_dynamic-update-slice_fusion.9
  371.1 16.7 %fusion.41 = f32[8,12,6,6,9,256]{5,1,4,3,2,0:T(8,128)} fusion(bf16[9,256,256,1,1,1]{2,1,0,5,4,3:T(8,128)(2,1)S(1)} %bitcast.412, bf16[8,12,6,6,256,1]{4,3,2,1,0,5:T(8,128)(2,1)S(1)} %bitcast.403), kind=kOutput, calls=%fused_computation.115 | convolution fusion | flops 4076863488 | bytes 34799616 | tf_op jit(solution)/shard_map/pd,tcd->ptc/dot_general | solution.py:97
  387.7 31.6 %slice_bitcast_fusion.8 = (f32[8,12,6,6,256]{4,1,3,2,0:T(8,128)}, f32[8,12,6,6,256]{4,1,3,2,0:T(8,128)}, f32[8,12,6,6,256]{4,1,3,2,0:T(8,128)}, f32[8,12,6,6,256...) fusion(f32[8,12,6,6,9,256]{5,1,4,3,2,0:T(8,128)} %fusion.41), kind=kLoop, calls=%fused_computation.48 | loop fusion | bytes 63700992 | tf_op jit(solution)/shard_map/squeeze | solution.py:103
  419.3 15.3 %bitcast_convert_fusion.1 = bf16[9,256,256]{1,2,0:T(8,128)(2,1)} fusion(bf16[8,12,8,8,9,256]{5,3,2,1,0,4:T(8,128)(2,1)} %bitcast_dynamic-update-slice_fusion.9, bf16[8,12,8,8,256,1]{4,1,3,0,2,5:T(8,128)(2,1)} %maximum_bitcast_fusion), kind=kOutput, calls=%fused_computation.109 | convolution fusion | flops 7248347136 | bytes 32636928 | tf_op jit(solution)/shard_map/pc,ptd->tcd/dot_general | solution.py:108
  434.7 5.4 %fusion.29 = bf16[1,8,12,6,6,256]{5,4,3,2,1,0:T(8,128)(2,1)S(1)} fusion(f32[1,8,12,6,6,256]{5,4,3,2,1,0:T(8,128)} %reshape.705, f32[8,12,6,6,1,256]{5,3,2,1,0,4:T(8,128)} %get-tuple-element.163), kind=kLoop, calls=%fused_computation.77 | loop fusion | flops 8847360 | bytes 8847360 | tf_op jit(solution)/shard_map/convert_element_type | solution.py:172
  440.0 3.1 copy.351
  443.1 15.0 %pad_add_fusion = f32[8,12,8,8,256]{4,1,3,2,0:T(8,128)S(1)} fusion(f32[8,12,6,6,256]{4,1,3,2,0:T(8,128)} %get-tuple-element.173, f32[8,12,6,6,256]{4,1,3,2,0:T(8,128)} %get-tuple-element.174, f32[8,12,6,6,256]{4,1,3,2,0:T(8,128)} %get-tuple-element.167, f32[8,12,6,6,256]{4,1,3,2,0:T(8,128)} %get-tuple-element.168, f32[8,12,6,6,256]{4,1,3,2,0:T(8,128)} %get-tuple-element.169, ...), kind=kLoop, calls=%fused_computation | loop fusion | flops 12582912 | bytes 38141952 | tf_op jit(solution)/shard_map/add | solution.py:104
  458.2 2.7 slice.581
  462.3 2.6 fusion.58
  464.9 2.5 fusion.60
  467.4 2.5 fusion.62
  470.0 3.3 add_bitcast_fusion
  473.4 3.8 copy.352
  477.2 46.8 %all-reduce.43.cloned.1.call-done = (bf16[576,256]{1,0:T(8,128)(2,1)}, bf16[576,256]{1,0:T(8,128)(2,1)}) async-done(((bf16[576,256]{1,0:T(8,128)(2,1)}, bf16[576,256]{1,0:T(8,128)(2,1)}), (bf16[576,256]{1,0:T(8,128)(2,1)}, bf16[576,256]{1,0:T(8,128)(2,1)})) %all-reduce.43.cloned.1.call-update) | async-done | bytes 589840 | tf_op jit(solution)/shard_map/psum | solution.py:211
  524.0 2.4 multiply_subtract_fusion.1
  526.5 2.4 multiply_subtract_fusion
  (138 shorter events, 51.3 us)
Async XLA Ops:
  7.2 28.6 %reduce-scatter.10.cloned.1.call-start = ((), (), s32[]{:S(2)}) async-start(), calls=%async_computation.7 | async-start | bytes 163840 | tf_op jit(solution)/shard_map/reduce_scatter | solution.py:204
  7.9 58.2 %copy-start.29 = (bf16[8]{0:T(256)(128)(2,1)}, bf16[8]{0:T(256)(128)(2,1)S(1)}, u32[]{:S(2)}) copy-start(bf16[8]{0:T(256)(128)(2,1)S(1)} %compare_convert_fusion) | copy-start | bytes 52
  7.9 5.9 %copy-start.11 = (f32[576,256]{1,0:T(8,128)S(1)}, f32[576,256]{1,0:T(8,128)}, u32[]{:S(2)}) copy-start(f32[576,256]{1,0:T(8,128)} %param.33) | copy-start | bytes 1769476
  7.9 6.7 %copy-start.13 = (f32[576,256]{1,0:T(8,128)S(1)}, f32[576,256]{1,0:T(8,128)}, u32[]{:S(2)}) copy-start(f32[576,256]{1,0:T(8,128)} %param.34) | copy-start | bytes 1769476
  7.9 7.6 %copy-start.6 = (bf16[1,8,12,6,6,256]{5,1,4,3,2,0:T(8,128)(2,1)S(1)}, bf16[1,8,12,6,6,256]{5,1,4,3,2,0:T(8,128)(2,1)}, u32[]{:S(2)}) copy-start(bf16[1,8,12,6,6,256]{5,1,4,3,2,0:T(8,128)(2,1)} %param.29) | copy-start | bytes 5308420
  13.0 3.6 copy-start.31
  13.8 84.2 %all-gather.3.cloned.1.call-start = ((), (), s32[]{:S(2)}) async-start(), calls=%async_computation.3 | async-start | bytes 1474560 | tf_op jit(solution)/shard_map/all_gather | solution.py:163
  14.6 129.8 %all-gather.5.cloned.1.call-start = ((), (), s32[]{:S(2)}) async-start(), calls=%async_computation.4 | async-start | bytes 1474560 | tf_op jit(solution)/shard_map/all_gather | solution.py:164
  15.4 454.6 %reduce-scatter.8.cloned.1.call-start = ((), (), s32[]{:S(2)}) async-start(), calls=%async_computation.6 | async-start | bytes 1474560 | tf_op jit(solution)/shard_map/reduce_scatter | solution.py:201
  16.6 2.7 copy-start.4
  16.6 42.9 %copy-start.26 = (f32[64,256]{1,0:T(8,128)S(1)}, f32[64,256]{1,0:T(8,128)}, u32[]{:S(2)}) copy-start(f32[64,256]{1,0:T(8,128)} %param.35) | copy-start | bytes 196612
  16.6 42.9 %copy-start.27 = (f32[64,256]{1,0:T(8,128)S(1)}, f32[64,256]{1,0:T(8,128)}, u32[]{:S(2)}) copy-start(f32[64,256]{1,0:T(8,128)} %param.40) | copy-start | bytes 196612
  16.6 42.9 %copy-start.28 = (f32[64,256]{1,0:T(8,128)S(1)}, f32[64,256]{1,0:T(8,128)}, u32[]{:S(2)}) copy-start(f32[64,256]{1,0:T(8,128)} %param.41) | copy-start | bytes 196612
  19.4 46.7 %copy-start = (bf16[1,8,12,6,6,256]{5,1,4,3,2,0:T(8,128)(2,1)S(1)}, bf16[1,8,12,6,6,256]{5,1,4,3,2,0:T(8,128)(2,1)}, u32[]{:S(2)}) copy-start(bf16[1,8,12,6,6,256]{5,1,4,3,2,0:T(8,128)(2,1)} %param.30) | copy-start | bytes 5308420
  60.2 5.8 %collective-permute-start = (bf16[1,64,256]{2,1,0:T(8,128)(2,1)S(1)}, bf16[1,64,256]{2,1,0:T(8,128)(2,1)S(1)}, u32[]{:S(2)}, u32[]{:S(2)}) collective-permute-start(bf16[1,64,256]{2,1,0:T(8,128)(2,1)S(1)} %bitcast.420), channel_id=1, source_target_pairs={{0,1},{1,0},{2,3},{3,2},{4,5},{5,4},{6,7},{7,6},{8,9},{9,8},{10,11... | collective-permute-start | bytes 98312 | tf_op jit(solution)/shard_map/ppermute | solution.py:22
  66.0 21.9 %collective-permute-start.1 = (bf16[2,64,256]{2,1,0:T(8,128)(2,1)S(1)}, bf16[2,64,256]{2,1,0:T(8,128)(2,1)S(1)}, u32[]{:S(2)}, u32[]{:S(2)}) collective-permute-start(bf16[2,64,256]{2,1,0:T(8,128)(2,1)S(1)} %get-tuple-element.196), channel_id=1, source_target_pairs={{0,2},{1,3},{2,0},{3,1},{4,6},{5,7},{6,4},{7,5},{8,10},{9,11},{10,... | collective-permute-start | bytes 196616 | tf_op jit(solution)/shard_map/ppermute | solution.py:22
  138.9 5.5 %copy-start.2 = (bf16[8,12,6,6,256]{4,3,2,1,0:T(8,128)(2,1)}, bf16[8,12,6,6,256]{4,3,2,1,0:T(8,128)(2,1)S(1)}, u32[]{:S(2)}) copy-start(bf16[8,12,6,6,256]{4,3,2,1,0:T(8,128)(2,1)S(1)} %get-tuple-element.164) | copy-start | bytes 5308420
  143.6 0.9 copy-start.15
  144.4 0.8 copy-start.17
  145.2 22.7 %copy-start.1 = (bf16[1,8,12,6,6,256]{5,1,4,3,2,0:T(8,128)(2,1)S(1)}, bf16[1,8,12,6,6,256]{5,1,4,3,2,0:T(8,128)(2,1)}, u32[]{:S(2)}) copy-start(bf16[1,8,12,6,6,256]{5,1,4,3,2,0:T(8,128)(2,1)} %param.30) | copy-start | bytes 5308420
  145.2 22.7 %copy-start.30 = (bf16[8]{0:T(256)(128)(2,1)S(1)}, bf16[8]{0:T(256)(128)(2,1)}, u32[]{:S(2)}) copy-start(bf16[8]{0:T(256)(128)(2,1)} %copy-done.29) | copy-start | bytes 52
  167.9 18.1 %copy-start.7 = (bf16[2304,256]{1,0:T(8,128)(2,1)S(1)}, bf16[2304,256]{1,0:T(8,128)(2,1)}, u32[]{:S(2)}) copy-start(bf16[2304,256]{1,0:T(8,128)(2,1)} %all-gather.5.cloned.1.call-done) | copy-start | bytes 3538948
  284.5 4.9 copy-start.3
  284.5 4.9 copy-start.16
  284.5 4.9 copy-start.18
  284.5 4.9 copy-start.19
  284.5 4.9 copy-start.20
  303.3 1.1 copy-start.10
  303.3 1.8 copy-start.9
  303.4 166.6 %reduce-scatter.6.cloned.1.call-start = ((), (), s32[]{:S(2)}) async-start(), calls=%async_computation.5 | async-start | bytes 1474560 | tf_op jit(solution)/shard_map/reduce_scatter | solution.py:198
  366.2 4.9 copy-start.8
  434.6 89.4 %all-reduce.43.cloned.1.call-start = ((), (), s32[]{:S(2)}) async-start(), calls=%async_computation.8 | async-start | bytes 1179648 | tf_op jit(solution)/shard_map/psum | solution.py:211
  460.9 9.1 %copy-start.5 = (bf16[8,12,6,6,256]{4,3,2,1,0:T(8,128)(2,1)S(1)}, bf16[8,12,6,6,256]{4,3,2,1,0:T(8,128)(2,1)}, u32[]{:S(2)}) copy-start(bf16[8,12,6,6,256]{4,3,2,1,0:T(8,128)(2,1)} %fusion.35) | copy-start | bytes 5308420
  460.9 9.1 %copy-start.25 = (bf16[256,256]{1,0:T(8,128)(2,1)S(1)}, bf16[256,256]{1,0:T(8,128)(2,1)}, u32[]{:S(2)}) copy-start(bf16[256,256]{1,0:T(8,128)(2,1)} %all_gather.13) | copy-start | bytes 393220
  473.3 50.8 %copy-start.12 = (f32[576,256]{1,0:T(8,128)S(1)}, f32[576,256]{1,0:T(8,128)}, u32[]{:S(2)}) copy-start(f32[576,256]{1,0:T(8,128)} %param.33) | copy-start | bytes 1769476
  473.3 50.7 %copy-start.21 = (f32[576,256]{1,0:T(8,128)S(1)}, f32[576,256]{1,0:T(8,128)}, u32[]{:S(2)}) copy-start(f32[576,256]{1,0:T(8,128)} %param.36) | copy-start | bytes 1769476
  473.3 50.7 %copy-start.22 = (f32[576,256]{1,0:T(8,128)S(1)}, f32[576,256]{1,0:T(8,128)}, u32[]{:S(2)}) copy-start(f32[576,256]{1,0:T(8,128)} %param.37) | copy-start | bytes 1769476
  473.3 53.2 %copy-start.14 = (f32[576,256]{1,0:T(8,128)S(1)}, f32[576,256]{1,0:T(8,128)}, u32[]{:S(2)}) copy-start(f32[576,256]{1,0:T(8,128)} %param.34) | copy-start | bytes 1769476
  473.3 53.2 %copy-start.23 = (f32[576,256]{1,0:T(8,128)S(1)}, f32[576,256]{1,0:T(8,128)}, u32[]{:S(2)}) copy-start(f32[576,256]{1,0:T(8,128)} %param.38) | copy-start | bytes 1769476
  473.4 53.1 %copy-start.24 = (f32[576,256]{1,0:T(8,128)S(1)}, f32[576,256]{1,0:T(8,128)}, u32[]{:S(2)}) copy-start(f32[576,256]{1,0:T(8,128)} %param.39) | copy-start | bytes 1769476
Sparse Core Ops, SparseCore 0:
  13.9 21.8 reduce-scatter.9
  38.0 28.9 all-gather.2
  69.3 31.9 all-gather.4
  303.5 27.7 reduce-scatter.7
  434.7 28.0 reduce-scatter.5
  470.1 53.8 all-reduce.42
